TPU v7x, 32 devices: a whole 2x2x4 slice. The times are simulated.
32 devices in a mesh: dom: 8 (over z, y), case: 4 (over x, core).
Axes of the slice: x: 2, y: 2, z: 4, core: 2. Of those that a mesh axis runs over, the one named last changes fastest.
Arguments:
- dual_ops: float32 [16, 1536, 1536], P('dom')
- modes: bfloat16 [16, 16, 1536], P('dom'), may hold values from -0.15625 to 0.15625
- coarse_rows: float32 [16, 8, 16, 16], P('dom'), may hold values from -1 to 1
- coarse_cols: int32 [16, 8], P('dom'), may hold values from 0 to 15, as said below
- row_perm: int32 [16, 1536], P('dom'), may hold values from 0 to 1535, each once within a row
- iface_size: int32 [16], P('dom'), may hold values from 256 to 768, as said below
- rhs: float32 [16, 768, 512], P('dom', None, 'case'), may hold values from -6 to 6
Outputs:
- solution: float32 [16, 768, 512], P('dom', None, 'case')
- residual: float32 [16, 768, 512], P('dom', None, 'case')
- history: float32 [4, 512], P(None, 'case')
- peak_norm: float32 [4], replicated
Inputs may be any that keep to these rules, and one draw needn't show every extreme that they name: `iface_size`: interfaces carry between 256 and 768 multipliers; both ends are reached in every draw. `coarse_cols`: for every subdomain s the first three entries are s, (s - 1) mod 16 and (s + 1) mod 16; the others are any subdomains, repeats allowed. `row_perm`: each row is a permutation of the local rows.
All inputs are finite; a program needn't handle non-finite values.
Results may differ from a plain program's by a relative error of at most 0.0056.
Values may be sent and summed in bfloat16 or wider, within the bound.
A program may use at most 192 MiB of HBM per device.

v0:
```python
import jax
import jax.numpy as jnp
from jax import lax
from jax.sharding import PartitionSpec as P

STEPS = 4
low_bound = 2.0
high_bound = 14.0
epsilon = 1e-06
highest = lax.Precision.HIGHEST


def from_behind(block, axis, distance):
    devices = range(lax.axis_size(axis))
    route = [((i - distance) % len(devices), i) for i in devices]
    return lax.ppermute(block, axis, route)


def slot_form(left_side, right_side):
    return jnp.concatenate([-left_side, right_side], axis=1)


def shards(dual_ops, modes, coarse_rows, coarse_cols, row_perm, iface_size, rhs):
    sub_count, half_width, case_count = rhs.shape
    dom_count = lax.axis_size("dom") * sub_count
    live_mask = (
        lax.broadcasted_iota(jnp.int32, (sub_count, half_width), 1) < iface_size[:, None]
    ).astype(jnp.float32)[:, :, None]
    slot_ops = jax.vmap(lambda matrix, ordering: matrix[ordering].T[ordering])(dual_ops, row_perm)
    slot_modes_low = jax.vmap(lambda block_rows, ordering: block_rows[:, ordering])(modes, row_perm)
    slot_modes = slot_modes_low.astype(jnp.float32)
    int_pack = jnp.concatenate([coarse_cols, iface_size[:, None]], axis=1)
    prior_ints = from_behind(int_pack[-1], "dom", 1)
    next_ints = from_behind(int_pack[0], "dom", -1)
    prior_modes = from_behind(slot_modes_low[-1], "dom", 1)
    next_modes = from_behind(slot_modes_low[0], "dom", -1)
    prior_blocks = from_behind(coarse_rows[-1], "dom", 1)
    next_blocks = from_behind(coarse_rows[0], "dom", -1)
    ext_ints = jnp.concatenate([prior_ints[None], int_pack, next_ints[None]], axis=0)
    block_count = coarse_cols.shape[1]
    ext_cols = ext_ints[:, :block_count]
    ext_size = ext_ints[:, block_count]
    ext_modes = jnp.concatenate(
        [prior_modes[None], slot_modes_low, next_modes[None]], axis=0
    ).astype(jnp.float32)
    ext_blocks = jnp.concatenate([prior_blocks[None], coarse_rows, next_blocks[None]], axis=0)
    ext_live = (
        lax.broadcasted_iota(jnp.int32, (sub_count + 2, half_width), 1) < ext_size[:, None]
    ).astype(jnp.float32)[:, :, None]

    def build_local(vector):
        prior_rim = from_behind(vector[-1], "dom", 1)
        left_side = jnp.concatenate([prior_rim[None], vector[:-1]], axis=0)
        return slot_form(left_side, vector)

    def select_columns(columns, all_coefficients):
        table = (
            columns[:, :, None] == lax.broadcasted_iota(jnp.int32, (1, 1, dom_count), 2)
        ).astype(jnp.float32)
        return jnp.einsum(
            "sqd,djc->sqjc", table, all_coefficients.astype(jnp.float32), precision=highest
        )

    def gather_coefficients(slot_rows):
        coefficients = jnp.einsum("sjn,snc->sjc", slot_modes, slot_rows, precision=highest).astype(
            jnp.bfloat16
        )
        return lax.all_gather(coefficients, "dom", axis=0, tiled=True)

    centre = 0.5 * (high_bound + low_bound)
    radius = 0.5 * (high_bound - low_bound)
    spread_ratio = centre / radius
    ratio_now = 1.0 / spread_ratio
    start_vector = rhs * live_mask
    picked = select_columns(coarse_cols, gather_coefficients(build_local(start_vector)))
    amounts = jnp.einsum("sqij,sqjc->sic", coarse_rows, picked, precision=highest)
    slot_rows = jnp.einsum("sjn,sjc->snc", slot_modes, amounts, precision=highest)
    lower_half = slot_rows[:, :half_width]
    upper_half = slot_rows[:, half_width:]
    later_rim = from_behind(lower_half[0], "dom", -1)
    following = jnp.concatenate([lower_half[1:], later_rim[None]], axis=0)
    residual = start_vector - (upper_half - following) * live_mask
    direction = residual / centre
    local_residual = build_local(residual)
    local_direction = local_residual / centre
    solution = jnp.zeros_like(rhs)
    norm_list = []
    for turn_index in range(STEPS):
        solution = solution + direction
        product = jnp.einsum("smn,smc->snc", slot_ops, local_direction, precision=highest)
        local_lower_half = product[:, :half_width]
        local_upper_half = product[:, half_width:]
        prior_upper = from_behind(local_upper_half[-1], "dom", 1)
        later_lower = from_behind(local_lower_half[0], "dom", -1)
        local_following = jnp.concatenate([local_lower_half[1:], later_lower[None]], axis=0)
        mapped = (local_upper_half - local_following) * live_mask
        first_value = (prior_upper - local_lower_half[0]) * ext_live[0]
        local_left_side = jnp.concatenate([first_value[None], mapped[:-1]], axis=0)
        mapped, local_mapped = (mapped, slot_form(local_left_side, mapped))
        wide_picked = select_columns(ext_cols, gather_coefficients(local_mapped))
        wide_amounts = jnp.einsum("sqij,sqjc->sic", ext_blocks, wide_picked, precision=highest)
        spread = jnp.einsum("sjn,sjc->snc", ext_modes, wide_amounts, precision=highest)
        lower_part = spread[:, :half_width]
        upper_part = spread[:, half_width:]
        joined = (upper_part[:-1] - lower_part[1:]) * ext_live[:-1]
        correction = joined[1:]
        local_correction = slot_form(joined[:-1], joined[1:])
        residual = residual - (mapped - correction)
        local_residual = local_residual - (local_mapped - local_correction)
        partial_value = jnp.sum(residual * residual, axis=(0, 1))
        norm_list.append(jnp.sqrt(lax.psum(partial_value, "dom") + epsilon))
        if turn_index + 1 < STEPS:
            ratio_next = 1.0 / (2.0 * spread_ratio - ratio_now)
            direction = ratio_next * ratio_now * direction + 2.0 * ratio_next / radius * residual
            local_direction = (
                ratio_next * ratio_now * local_direction
                + 2.0 * ratio_next / radius * local_residual
            )
            ratio_now = ratio_next
    history = jnp.stack(norm_list)
    peak_norm = lax.pmax(jnp.max(history, axis=1), "case")
    return (solution, residual, history, peak_norm)


def solution(mesh):
    in_specs = (
        P("dom", None, None),
        P("dom", None, None),
        P("dom", None, None, None),
        P("dom", None),
        P("dom", None),
        P("dom"),
        P("dom", None, "case"),
    )
    out_specs = (P("dom", None, "case"), P("dom", None, "case"), P(None, "case"), P())
    return jax.shard_map(shards, mesh=mesh, in_specs=in_specs, out_specs=out_specs, check_vma=False)
```

profile of v0, /device:TPU:0, one launch (start us, length us, event | category | flops | bytes accessed | tf_op | source)
XLA Modules:
  0.0 592.4 jit_solution(7699816429259120163)
XLA Ops:
  7.3 16.5 %gather_fusion = bf16[3072,16]{1,0:T(8,128)(2,1)S(1)} fusion(bf16[2,16,1536]{1,2,0:T(8,128)(2,1)S(1)} %copy.28, s32[3072]{0:T(1024)S(1)} %reshape.35), kind=kCustom, calls=%fused_computation | custom fusion | bytes 221184 | tf_op jit(solution)/shard_map/vmap()/gather | solution.py:30
  24.8 30.9 %all_gather.15 = bf16[16,16,128]{2,1,0:T(8,128)(2,1)S(1)} all-gather(bf16[2,16,128]{2,1,0:T(8,128)(2,1)S(1)} %fusion.33), channel_id=1, replica_groups=mesh['dom'=8,'case'=4] {'dom'}, dimensions={0}, use_global_device_ids=true | all-gather | bytes 73728 | tf_op jit(solution)/shard_map/all_gather | solution.py:68
  66.2 68.1 %gather_fusion.1 = f32[3072,1536]{1,0:T(8,128)} fusion(f32[2,1536,1536]{2,1,0:T(8,128)} %param.7, s32[3072]{0:T(1024)S(1)} %reshape.35), kind=kCustom, calls=%fused_computation.1 | custom fusion | bytes 37773312 | tf_op jit(solution)/shard_map/vmap()/gather | solution.py:29
  134.3 18.7 %copy.34 = f32[2,1536,1536]{1,2,0:T(8,128)} copy(f32[2,1536,1536]{2,1,0:T(8,128)} %bitcast.153) | data formatting | bytes 37748736 | tf_op jit(solution)/shard_map/vmap()/gather | solution.py:29
  153.0 68.1 %gather_fusion.2 = f32[3072,1536]{1,0:T(8,128)} fusion(f32[2,1536,1536]{2,1,0:T(8,128)} %bitcast.146, s32[3072]{0:T(1024)S(1)} %reshape.35), kind=kCustom, calls=%fused_computation.2 | custom fusion | bytes 37773312 | tf_op jit(solution)/shard_map/vmap()/gather | solution.py:29
  224.0 4.5 collective-permute-start.5
  228.6 5.4 collective-permute-done.2
  234.1 32.9 %fusion.18 = f32[2,1536,128]{2,1,0:T(8,128)S(1)} fusion(f32[2,1536,1536]{2,1,0:T(8,128)} %bitcast.147, f32[2,768,128]{2,1,0:T(8,128)S(1)} %fusion.44, f32[2,768,128]{2,1,0:T(8,128)S(1)} %maximum_negate_fusion.1), kind=kOutput, calls=%fused_computation.29 | convolution fusion | flops 7248543744 | bytes 22020096 | tf_op jit(solution)/shard_map/smn,smc->snc/dot_general | solution.py:90
  270.1 5.5 collective-permute-done.3
  275.9 4.6 collective-permute-done.10
  281.7 30.7 %all_gather.16 = bf16[16,16,128]{2,1,0:T(8,128)(2,1)S(1)} all-gather(bf16[2,16,128]{2,1,0:T(8,128)(2,1)S(1)} %fusion.27), channel_id=1, replica_groups=mesh['dom'=8,'case'=4] {'dom'}, dimensions={0}, use_global_device_ids=true | all-gather | bytes 73728 | tf_op jit(solution)/shard_map/all_gather | solution.py:68
  317.5 31.7 %fusion.115 = f32[2,1536,128]{2,1,0:T(8,128)S(1)} fusion(f32[2,1536,1536]{2,1,0:T(8,128)S(1)} %bitcast.150, f32[2,1536,128]{2,1,0:T(8,128)S(1)} %multiply_add_fusion.1), kind=kOutput, calls=%fused_computation.185 | convolution fusion | flops 7247757312 | bytes 22020096 | tf_op jit(solution)/shard_map/smn,smc->snc/dot_general | solution.py:90
  351.3 5.8 collective-permute-done.11
  362.7 30.5 %all_gather.17 = bf16[16,16,128]{2,1,0:T(8,128)(2,1)S(1)} all-gather(bf16[2,16,128]{2,1,0:T(8,128)(2,1)S(1)} %fusion.28), channel_id=1, replica_groups=mesh['dom'=8,'case'=4] {'dom'}, dimensions={0}, use_global_device_ids=true | all-gather | bytes 73728 | tf_op jit(solution)/shard_map/all_gather | solution.py:68
  399.7 33.1 %fusion.20 = f32[2,1536,128]{2,1,0:T(8,128)} fusion(f32[2,1536,1536]{2,1,0:T(8,128)S(1)} %bitcast.151, f32[2,1536,128]{2,1,0:T(8,128)} %fusion.5, f32[2,1536,128]{2,1,0:T(8,128)S(1)} %multiply_add_fusion.1), kind=kOutput, calls=%fused_computation.31 | convolution fusion | flops 7248936960 | bytes 23592960 | tf_op jit(solution)/shard_map/smn,smc->snc/dot_general | solution.py:90
  436.3 5.8 collective-permute-done.13
  442.6 4.3 collective-permute-done.14
  448.1 30.5 %all_gather.18 = bf16[16,16,128]{2,1,0:T(8,128)(2,1)S(1)} all-gather(bf16[2,16,128]{2,1,0:T(8,128)(2,1)S(1)} %fusion.29), channel_id=1, replica_groups=mesh['dom'=8,'case'=4] {'dom'}, dimensions={0}, use_global_device_ids=true | all-gather | bytes 73728 | tf_op jit(solution)/shard_map/all_gather | solution.py:68
  484.1 32.5 %fusion.9 = f32[2,1536,128]{2,1,0:T(8,128)S(1)} fusion(f32[2,1536,1536]{2,1,0:T(8,128)S(1)} %bitcast.152, f32[2,1536,128]{2,1,0:T(8,128)S(1)} %copy-done, f32[2,768,128]{2,1,0:T(8,128)} %get-tuple-element.35, f32[2,768,128]{2,1,0:T(8,128)} %get-tuple-element.34, f32[2,1536,128]{2,1,0:T(8,128)S(1)} %multiply_add_fusion.1, f32[2,768,128]{2,1,0:T(8,128)S(1)} %fusion.40, ...), kind=kOutput, calls=%fused_computation.19 | convolution fusion | flops 7251689472 | bytes 26738688 | tf_op jit(solution)/shard_map/smn,smc->snc/dot_general | solution.py:90
  518.8 5.8 collective-permute-done.15
  525.0 4.0 collective-permute-done.16
  530.2 30.5 %all_gather.19 = bf16[16,16,128]{2,1,0:T(8,128)(2,1)S(1)} all-gather(bf16[2,16,128]{2,1,0:T(8,128)(2,1)S(1)} %fusion.30), channel_id=1, replica_groups=mesh['dom'=8,'case'=4] {'dom'}, dimensions={0}, use_global_device_ids=true | all-gather | bytes 73728 | tf_op jit(solution)/shard_map/all_gather | solution.py:68
  566.3 19.1 %all-reduce = (f32[128]{0:T(128)S(1)}, f32[128]{0:T(128)S(1)}, f32[128]{0:T(128)S(1)}, f32[128]{0:T(128)S(1)}) all-reduce(f32[128]{0:T(128)S(1)} %get-tuple-element.16, f32[128]{0:T(128)S(1)} %get-tuple-element.14, f32[128]{0:T(128)S(1)} %get-tuple-element.12, f32[128]{0:T(128)S(1)} %get-tuple-element.10), channel_id=1, replica_groups=mesh['dom'=8,'case'=4] {'dom'}, use_global_device_ids=true, to_apply=%region_7.0 | all-reduce | flops 512 | bytes 4096 | tf_op jit(solution)/shard_map/psum | solution.py:111
  586.0 6.2 %pmax.7 = f32[4]{0:T(128)} all-reduce(f32[4]{0:T(128)S(1)} %get-tuple-element.8), channel_id=1, replica_groups=mesh['dom'=8,'case'=4] {'case'}, use_global_device_ids=true, to_apply=%region_9.0 | all-reduce | flops 4 | bytes 32 | tf_op jit(solution)/shard_map/pmax | solution.py:121
  (142 shorter events, 65.3 us)
Async XLA Ops:
  3.6 20.2 %collective-permute-start = (f32[768,128]{1,0:T(8,128)}, f32[768,128]{1,0:T(8,128)S(1)}, u32[]{:S(2)}, u32[]{:S(2)}) collective-permute-start(f32[768,128]{1,0:T(8,128)} %get-tuple-element.43), channel_id=1, source_target_pairs={{28,0},{0,4},{4,8},{8,12},{12,16},{16,20},{20,24},{24,28},{29,1},{... | collective-permute-start | bytes 1179656 | tf_op jit(solution)/shard_map/ppermute | solution.py:16
  7.0 16.8 %copy-start.13 = (s32[2,8]{1,0:T(2,128)S(1)}, s32[2,8]{1,0:T(2,128)}, u32[]{:S(2)}) copy-start(s32[2,8]{1,0:T(2,128)} %param.10) | copy-start | bytes 196
  57.9 163.1 %collective-permute-start.1 = (f32[768,128]{1,0:T(8,128)S(1)}, f32[768,128]{1,0:T(8,128)S(1)}, u32[]{:S(2)}, u32[]{:S(2)}) collective-permute-start(f32[768,128]{1,0:T(8,128)S(1)} %get-tuple-element.33), channel_id=1, source_target_pairs={{4,0},{8,4},{12,8},{16,12},{20,16},{24,20},{28,24},{0,28},{5,1},{9... | collective-permute-start | bytes 1179656 | tf_op jit(solution)/shard_map/ppermute | solution.py:16
  60.6 163.5 %collective-permute-start.9 = (s32[9]{0:T(128)S(1)}, s32[9]{0:T(128)S(1)}, u32[]{:S(2)}, u32[]{:S(2)}) collective-permute-start(s32[9]{0:T(128)S(1)} %get-tuple-element.50), channel_id=1, source_target_pairs={{4,0},{8,4},{12,8},{16,12},{20,16},{24,20},{28,24},{0,28},{5,1},{9... | collective-permute-start | bytes 116 | tf_op jit(solution)/shard_map/ppermute | solution.py:16
  60.6 168.0 %collective-permute-start.8 = (s32[9]{0:T(128)S(1)}, s32[9]{0:T(128)S(1)}, u32[]{:S(2)}, u32[]{:S(2)}) collective-permute-start(s32[9]{0:T(128)S(1)} %get-tuple-element.49), channel_id=1, source_target_pairs={{28,0},{0,4},{4,8},{8,12},{12,16},{16,20},{20,24},{24,28},{29,1},{... | collective-permute-start | bytes 116 | tf_op jit(solution)/shard_map/ppermute | solution.py:16
  63.2 249.4 %collective-permute-start.7 = (f32[8,16,16]{2,1,0:T(8,128)}, f32[8,16,16]{2,1,0:T(8,128)S(1)}, u32[]{:S(2)}, u32[]{:S(2)}) collective-permute-start(f32[8,16,16]{2,1,0:T(8,128)} %get-tuple-element.46), channel_id=1, source_target_pairs={{4,0},{8,4},{12,8},{16,12},{20,16},{24,20},{28,24},{0,28},{5,1},{9... | collective-permute-start | bytes 24584 | tf_op jit(solution)/shard_map/ppermute | solution.py:16
  66.0 246.7 %collective-permute-start.6 = (f32[8,16,16]{2,1,0:T(8,128)}, f32[8,16,16]{2,1,0:T(8,128)S(1)}, u32[]{:S(2)}, u32[]{:S(2)}) collective-permute-start(f32[8,16,16]{2,1,0:T(8,128)} %get-tuple-element.45), channel_id=1, source_target_pairs={{28,0},{0,4},{4,8},{8,12},{12,16},{16,20},{20,24},{24,28},{29,1},{... | collective-permute-start | bytes 24584 | tf_op jit(solution)/shard_map/ppermute | solution.py:16
  223.5 10.6 %collective-permute-start.2 = (f32[768,128]{1,0:T(8,128)S(1)}, f32[768,128]{1,0:T(8,128)S(1)}, u32[]{:S(2)}, u32[]{:S(2)}) collective-permute-start(f32[768,128]{1,0:T(8,128)S(1)} %get-tuple-element.41), channel_id=1, source_target_pairs={{28,0},{0,4},{4,8},{8,12},{12,16},{16,20},{20,24},{24,28},{29,1},{... | collective-permute-start | bytes 1179656 | tf_op jit(solution)/shard_map/ppermute | solution.py:16
  224.0 89.3 %collective-permute-start.5 = (bf16[16,1536]{1,0:T(8,128)(2,1)S(1)}, bf16[16,1536]{1,0:T(8,128)(2,1)S(1)}, u32[]{:S(2)}, u32[]{:S(2)}) collective-permute-start(bf16[16,1536]{1,0:T(8,128)(2,1)S(1)} %get-tuple-element.48), channel_id=1, source_target_pairs={{4,0},{8,4},{12,8},{16,12},{20,16},{24,20},{28,24},{0,28},{5,1},{9... | collective-permute-start | bytes 147464 | tf_op jit(solution)/shard_map/ppermute | solution.py:16
  234.1 83.4 %slice-start = ((s8[18874368]{0:T(1024)(128)(4,1)}), s8[4194304]{0:T(1024)(128)(4,1)S(1)}, s32[]{:S(2)}) async-start(s8[18874368]{0:T(1024)(128)(4,1)} %bitcast.148), calls=%async_computation | async-start | bytes 8388608
  234.1 83.4 %slice-start.1 = ((s8[18874368]{0:T(1024)(128)(4,1)}), s8[4194304]{0:T(1024)(128)(4,1)S(1)}, s32[]{:S(2)}) async-start(s8[18874368]{0:T(1024)(128)(4,1)} %bitcast.148), calls=%async_computation.1 | async-start | bytes 8388608
  234.1 83.4 %slice-start.2 = ((s8[18874368]{0:T(1024)(128)(4,1)}), s8[4194304]{0:T(1024)(128)(4,1)S(1)}, s32[]{:S(2)}) async-start(s8[18874368]{0:T(1024)(128)(4,1)} %bitcast.148), calls=%async_computation.2 | async-start | bytes 8388608
  267.1 8.4 %collective-permute-start.3 = (f32[768,128]{1,0:T(8,128)S(1)}, f32[768,128]{1,0:T(8,128)S(1)}, u32[]{:S(2)}, u32[]{:S(2)}) collective-permute-start(f32[768,128]{1,0:T(8,128)S(1)} %get-tuple-element.30), channel_id=1, source_target_pairs={{4,0},{8,4},{12,8},{16,12},{20,16},{24,20},{28,24},{0,28},{5,1},{9... | collective-permute-start | bytes 1179656 | tf_op jit(solution)/shard_map/ppermute | solution.py:16
  269.9 10.6 %collective-permute-start.10 = (f32[768,128]{1,0:T(8,128)S(1)}, f32[768,128]{1,0:T(8,128)S(1)}, u32[]{:S(2)}, u32[]{:S(2)}) collective-permute-start(f32[768,128]{1,0:T(8,128)S(1)} %get-tuple-element.29), channel_id=1, source_target_pairs={{28,0},{0,4},{4,8},{8,12},{12,16},{16,20},{20,24},{24,28},{29,1},{... | collective-permute-start | bytes 1179656 | tf_op jit(solution)/shard_map/ppermute | solution.py:16
  275.5 37.8 %collective-permute-start.4 = (bf16[16,1536]{1,0:T(8,128)(2,1)S(1)}, bf16[16,1536]{1,0:T(8,128)(2,1)S(1)}, u32[]{:S(2)}, u32[]{:S(2)}) collective-permute-start(bf16[16,1536]{1,0:T(8,128)(2,1)S(1)} %get-tuple-element.47), channel_id=1, source_target_pairs={{28,0},{0,4},{4,8},{8,12},{12,16},{16,20},{20,24},{24,28},{29,1},{... | collective-permute-start | bytes 147464 | tf_op jit(solution)/shard_map/ppermute | solution.py:16
  280.8 36.7 %slice-start.3 = ((s8[18874368]{0:T(1024)(128)(4,1)}), s8[4194304]{0:T(1024)(128)(4,1)S(1)}, s32[]{:S(2)}) async-start(s8[18874368]{0:T(1024)(128)(4,1)} %bitcast.148), calls=%async_computation.3 | async-start | bytes 8388608
  349.3 7.9 %collective-permute-start.11 = (f32[768,128]{1,0:T(8,128)S(1)}, f32[768,128]{1,0:T(8,128)S(1)}, u32[]{:S(2)}, u32[]{:S(2)}) collective-permute-start(f32[768,128]{1,0:T(8,128)S(1)} %get-tuple-element.27), channel_id=1, source_target_pairs={{4,0},{8,4},{12,8},{16,12},{20,16},{24,20},{28,24},{0,28},{5,1},{9... | collective-permute-start | bytes 1179656 | tf_op jit(solution)/shard_map/ppermute | solution.py:16
  350.9 10.6 %collective-permute-start.12 = (f32[768,128]{1,0:T(8,128)S(1)}, f32[768,128]{1,0:T(8,128)S(1)}, u32[]{:S(2)}, u32[]{:S(2)}) collective-permute-start(f32[768,128]{1,0:T(8,128)S(1)} %get-tuple-element.26), channel_id=1, source_target_pairs={{28,0},{0,4},{4,8},{8,12},{12,16},{16,20},{20,24},{24,28},{29,1},{... | collective-permute-start | bytes 1179656 | tf_op jit(solution)/shard_map/ppermute | solution.py:16
  432.8 9.4 %copy-start.1 = (f32[2,1536,128]{2,1,0:T(8,128)S(1)}, f32[2,1536,128]{2,1,0:T(8,128)}, u32[]{:S(2)}) copy-start(f32[2,1536,128]{2,1,0:T(8,128)} %fusion.20) | copy-start | bytes 4718596
  434.3 7.9 %collective-permute-start.13 = (f32[768,128]{1,0:T(8,128)S(1)}, f32[768,128]{1,0:T(8,128)S(1)}, u32[]{:S(2)}, u32[]{:S(2)}) collective-permute-start(f32[768,128]{1,0:T(8,128)S(1)} %get-tuple-element.24), channel_id=1, source_target_pairs={{4,0},{8,4},{12,8},{16,12},{20,16},{24,20},{28,24},{0,28},{5,1},{9... | collective-permute-start | bytes 1179656 | tf_op jit(solution)/shard_map/ppermute | solution.py:16
  436.3 10.6 %collective-permute-start.14 = (f32[768,128]{1,0:T(8,128)S(1)}, f32[768,128]{1,0:T(8,128)S(1)}, u32[]{:S(2)}, u32[]{:S(2)}) collective-permute-start(f32[768,128]{1,0:T(8,128)S(1)} %get-tuple-element.23), channel_id=1, source_target_pairs={{28,0},{0,4},{4,8},{8,12},{12,16},{16,20},{20,24},{24,28},{29,1},{... | collective-permute-start | bytes 1179656 | tf_op jit(solution)/shard_map/ppermute | solution.py:16
  447.2 32.4 %copy-start.7 = (f32[2,768,128]{2,1,0:T(8,128)}, f32[2,768,128]{2,1,0:T(8,128)S(1)}, u32[]{:S(2)}) copy-start(f32[2,768,128]{2,1,0:T(8,128)S(1)} %maximum_negate_fusion.4) | copy-start | bytes 2359300
  516.7 7.9 %collective-permute-start.15 = (f32[768,128]{1,0:T(8,128)S(1)}, f32[768,128]{1,0:T(8,128)S(1)}, u32[]{:S(2)}, u32[]{:S(2)}) collective-permute-start(f32[768,128]{1,0:T(8,128)S(1)} %get-tuple-element.21), channel_id=1, source_target_pairs={{4,0},{8,4},{12,8},{16,12},{20,16},{24,20},{28,24},{0,28},{5,1},{9... | collective-permute-start | bytes 1179656 | tf_op jit(solution)/shard_map/ppermute | solution.py:16
  518.5 10.5 %collective-permute-start.16 = (f32[768,128]{1,0:T(8,128)S(1)}, f32[768,128]{1,0:T(8,128)S(1)}, u32[]{:S(2)}, u32[]{:S(2)}) collective-permute-start(f32[768,128]{1,0:T(8,128)S(1)} %get-tuple-element.20), channel_id=1, source_target_pairs={{28,0},{0,4},{4,8},{8,12},{12,16},{16,20},{20,24},{24,28},{29,1},{... | collective-permute-start | bytes 1179656 | tf_op jit(solution)/shard_map/ppermute | solution.py:16
  (13 other events, 29.9 us)
where the time goes:
time: 601 us; the launch traced here: 592 us
  local copies, waits for them, and re-layouts  181 us (30%)
  blocking collectives  178 us (30%)
  matrix products  146 us (24%)
  waiting for transfers between devices  45.1 us (8%)
  starting transfers between devices  24.3 us (4%)
  other arithmetic  16.3 us (3%)
    gather x3, local copies, waits for them, and re-layouts, shards(): matrix[ordering].T[ordering]  155 us
    all_gather x5, blocking collectives, gather_coefficients(): return lax.all_gather(coefficients, 'dom', axis=0, tiled=True)  153 us
    dot_general x4, matrix products, shards(): jnp.einsum('smn,smc->snc', slot_ops, local_direction, precision=highest)  130 us
    ppermute x17, waiting for transfers between devices, from_behind(): return lax.ppermute(block, axis, route)  45.1 us
    ppermute x17, starting transfers between devices, from_behind(): return lax.ppermute(block, axis, route)  24.3 us
    psum x1, blocking collectives, shards(): norm_list.append(jnp.sqrt(lax.psum(partial_value, 'dom') + epsilon))  19.1 us
    gather x3, local copies, waits for them, and re-layouts, shards(): block_rows[:, ordering]  16.7 us
  transfers between devices with their start and end apart: 17, of which 9 were waited for; matrix products, arithmetic and copies ran while one was open for 36% of the time, Pallas kernels for 0%

commit v1 on v0

--- a/solution.py
+++ b/solution.py
@@ -8,6 +8,19 @@
 high_bound = 14.0
 epsilon = 1e-06
 highest = lax.Precision.HIGHEST
+
+
+def ring_gather(x, axis, dim):
+    ways = lax.axis_size(axis)
+    up = [(d, (d + 1) % ways) for d in range(ways)]
+    down = [(d, (d - 1) % ways) for d in range(ways)]
+    earlier, later = ([x], [x])
+    for _ in range(ways // 2):
+        earlier.append(lax.ppermute(earlier[-1], axis, up))
+    for _ in range((ways - 1) // 2):
+        later.append(lax.ppermute(later[-1], axis, down))
+    line = jnp.concatenate([*earlier[::-1], *later[1:]], axis=dim)
+    return jnp.roll(line, (lax.axis_index(axis) - ways // 2) * x.shape[dim], axis=dim)
 
 
 def from_behind(block, axis, distance):
@@ -65,7 +78,7 @@
         coefficients = jnp.einsum("sjn,snc->sjc", slot_modes, slot_rows, precision=highest).astype(
             jnp.bfloat16
         )
-        return lax.all_gather(coefficients, "dom", axis=0, tiled=True)
+        return ring_gather(coefficients, "dom", 0)
 
     centre = 0.5 * (high_bound + low_bound)
     radius = 0.5 * (high_bound - low_bound)

time: 601 us -> 598 us (level)
  blocking collectives: 178 us -> 28 us
  starting transfers between devices: 24.3 us -> 112 us
  waiting for transfers between devices: 45.1 us -> 98.3 us
    all_gather x5 -> x0, blocking collectives: 153 us -> none  [gather_coefficients(): return lax.all_gather(coefficients, 'dom', axis=0, tiled=True)]
    ppermute x0 -> x35, starting transfers between devices: none -> 71 us  [the longest x15 69.2 us: ring_gather(): later.append(lax.ppermute(later[-1], axis, down))]
    ppermute x0 -> x35, waiting for transfers between devices: none -> 53.3 us  [the longest x20 53.3 us: ring_gather(): earlier.append(lax.ppermute(earlier[-1], axis, up))]
    ppermute x17, starting transfers between devices: 24.3 us -> 41 us  [from_behind(): return lax.ppermute(block, axis, route)]
  transfers between devices with their start and end apart: 17 -> 52, of which waited for: 9 -> 28; matrix products, arithmetic and copies ran while one was open for 36% -> 30% of each run, Pallas kernels for 0% -> 0%
where the time goes in v1:
time: 598 us; the launch traced here: 589 us
  local copies, waits for them, and re-layouts  185 us (31%)
  matrix products  148 us (25%)
  starting transfers between devices  112 us (19%)
  waiting for transfers between devices  98.3 us (16%)
  blocking collectives  28 us (5%)
  other arithmetic  16.1 us (3%)
    gather x3, local copies, waits for them, and re-layouts, shards(): matrix[ordering].T[ordering]  155 us
    dot_general x4, matrix products, shards(): jnp.einsum('smn,smc->snc', slot_ops, local_direction, precision=highest)  132 us
    ppermute x15, starting transfers between devices, ring_gather(): later.append(lax.ppermute(later[-1], axis, down))  69.2 us
    ppermute x20, waiting for transfers between devices, ring_gather(): earlier.append(lax.ppermute(earlier[-1], axis, up))  53.3 us
    ppermute x17, waiting for transfers between devices, from_behind(): return lax.ppermute(block, axis, route)  45 us
    ppermute x17, starting transfers between devices, from_behind(): return lax.ppermute(block, axis, route)  41 us
    psum x1, blocking collectives, shards(): norm_list.append(jnp.sqrt(lax.psum(partial_value, 'dom') + epsilon))  21.8 us
    gather x3, local copies, waits for them, and re-layouts, shards(): block_rows[:, ordering]  16.7 us
  transfers between devices with their start and end apart: 52, of which 28 were waited for; matrix products, arithmetic and copies ran while one was open for 30% of the time, Pallas kernels for 0%

profile of v1, /device:TPU:0, one launch (start us, length us, event | category | flops | bytes accessed | tf_op | source)
XLA Modules:
  0.0 589.0 jit_solution(4666028566387051927)
XLA Ops:
  7.0 16.5 %gather_fusion = bf16[3072,16]{1,0:T(8,128)(2,1)S(1)} fusion(bf16[2,16,1536]{1,2,0:T(8,128)(2,1)S(1)} %copy.18, s32[3072]{0:T(1024)S(1)} %reshape.35), kind=kCustom, calls=%fused_computation | custom fusion | bytes 221184 | tf_op jit(solution)/shard_map/vmap()/gather | solution.py:43
  26.1 4.8 collective-permute-done.1
  57.3 5.2 collective-permute-done.8
  65.1 5.3 collective-permute-start.16
  70.4 68.1 %gather_fusion.1 = f32[3072,1536]{1,0:T(8,128)} fusion(f32[2,1536,1536]{2,1,0:T(8,128)} %param.9, s32[3072]{0:T(1024)S(1)} %reshape.35), kind=kCustom, calls=%fused_computation.1 | custom fusion | bytes 37773312 | tf_op jit(solution)/shard_map/vmap()/gather | solution.py:42
  138.4 18.7 %copy.22 = f32[2,1536,1536]{1,2,0:T(8,128)} copy(f32[2,1536,1536]{2,1,0:T(8,128)} %bitcast.148) | data formatting | bytes 37748736 | tf_op jit(solution)/shard_map/vmap()/gather | solution.py:42
  157.1 68.1 %gather_fusion.2 = f32[3072,1536]{1,0:T(8,128)} fusion(f32[2,1536,1536]{2,1,0:T(8,128)} %bitcast.141, s32[3072]{0:T(1024)S(1)} %reshape.35), kind=kCustom, calls=%fused_computation.2 | custom fusion | bytes 37773312 | tf_op jit(solution)/shard_map/vmap()/gather | solution.py:42
  225.4 33.0 %fusion.18 = f32[2,1536,128]{2,1,0:T(8,128)S(1)} fusion(f32[2,1536,1536]{2,1,0:T(8,128)} %bitcast.142, f32[2,768,128]{2,1,0:T(8,128)S(1)} %fusion.44, f32[2,768,128]{2,1,0:T(8,128)S(1)} %maximum_negate_fusion.1), kind=kOutput, calls=%fused_computation.29 | convolution fusion | flops 7248543744 | bytes 22020096 | tf_op jit(solution)/shard_map/smn,smc->snc/dot_general | solution.py:103
  258.5 4.8 collective-permute-start.10
  263.7 6.2 %collective-permute-done.10 = f32[768,128]{1,0:T(8,128)S(1)} collective-permute-done((f32[768,128]{1,0:T(8,128)S(1)}, f32[768,128]{1,0:T(8,128)S(1)}, u32[]{:S(2)}, u32[]{:S(2)}) %collective-permute-start.10) | collective-permute-done | bytes 393248 | tf_op jit(solution)/shard_map/ppermute | solution.py:29
  275.4 6.4 %collective-permute-done.18 = bf16[2,16,128]{2,1,0:T(8,128)(2,1)S(1)} collective-permute-done((bf16[2,16,128]{2,1,0:T(8,128)(2,1)S(1)}, bf16[2,16,128]{2,1,0:T(8,128)(2,1)S(1)}, u32[]{:S(2)}, u32[]{:S(2)}) %collective-permute-start.18) | collective-permute-done | bytes 8224 | tf_op jit(solution)/shard_map/ppermute | solution.py:19
  316.7 33.4 %fusion.120 = f32[2,1536,128]{2,1,0:T(8,128)S(1)} fusion(f32[2,1536,1536]{2,1,0:T(8,128)} %bitcast.143, f32[2,1536,128]{2,1,0:T(8,128)S(1)} %multiply_add_fusion.1), kind=kOutput, calls=%fused_computation.240 | convolution fusion | flops 7247757312 | bytes 22020096 | tf_op jit(solution)/shard_map/smn,smc->snc/dot_general | solution.py:103
  354.4 5.3 collective-permute-done.25
  360.1 4.9 collective-permute-done.26
  366.3 6.4 %collective-permute-done.27 = bf16[2,16,128]{2,1,0:T(8,128)(2,1)S(1)} collective-permute-done((bf16[2,16,128]{2,1,0:T(8,128)(2,1)S(1)}, bf16[2,16,128]{2,1,0:T(8,128)(2,1)S(1)}, u32[]{:S(2)}, u32[]{:S(2)}) %collective-permute-start.27) | collective-permute-done | bytes 8224 | tf_op jit(solution)/shard_map/ppermute | solution.py:19
  397.7 33.2 %fusion.20 = f32[2,1536,128]{2,1,0:T(8,128)} fusion(f32[2,1536,1536]{2,1,0:T(8,128)S(1)} %bitcast.146, f32[2,1536,128]{2,1,0:T(8,128)} %fusion.5, f32[2,1536,128]{2,1,0:T(8,128)S(1)} %multiply_add_fusion.1), kind=kOutput, calls=%fused_computation.31 | convolution fusion | flops 7248936960 | bytes 23592960 | tf_op jit(solution)/shard_map/smn,smc->snc/dot_general | solution.py:103
  437.0 5.3 collective-permute-done.34
  442.7 5.0 collective-permute-done.35
  448.9 6.3 %collective-permute-done.36 = bf16[2,16,128]{2,1,0:T(8,128)(2,1)S(1)} collective-permute-done((bf16[2,16,128]{2,1,0:T(8,128)(2,1)S(1)}, bf16[2,16,128]{2,1,0:T(8,128)(2,1)S(1)}, u32[]{:S(2)}, u32[]{:S(2)}) %collective-permute-start.36) | collective-permute-done | bytes 8224 | tf_op jit(solution)/shard_map/ppermute | solution.py:19
  480.0 32.5 %fusion.9 = f32[2,1536,128]{2,1,0:T(8,128)S(1)} fusion(f32[2,1536,1536]{2,1,0:T(8,128)S(1)} %bitcast.147, f32[2,1536,128]{2,1,0:T(8,128)S(1)} %copy-done.2, f32[2,768,128]{2,1,0:T(8,128)} %get-tuple-element.36, f32[2,768,128]{2,1,0:T(8,128)} %get-tuple-element.35, f32[2,1536,128]{2,1,0:T(8,128)S(1)} %multiply_add_fusion.1, f32[2,768,128]{2,1,0:T(8,128)S(1)} %fusion.40, ...), kind=kOutput, calls=%fused_computation.19 | convolution fusion | flops 7251689472 | bytes 26738688 | tf_op jit(solution)/shard_map/smn,smc->snc/dot_general | solution.py:103
  517.3 5.4 collective-permute-done.43
  529.0 6.3 %collective-permute-done.45 = bf16[2,16,128]{2,1,0:T(8,128)(2,1)S(1)} collective-permute-done((bf16[2,16,128]{2,1,0:T(8,128)(2,1)S(1)}, bf16[2,16,128]{2,1,0:T(8,128)(2,1)S(1)}, u32[]{:S(2)}, u32[]{:S(2)}) %collective-permute-start.45) | collective-permute-done | bytes 8224 | tf_op jit(solution)/shard_map/ppermute | solution.py:19
  560.1 21.8 %all-reduce = (f32[128]{0:T(128)S(1)}, f32[128]{0:T(128)S(1)}, f32[128]{0:T(128)S(1)}, f32[128]{0:T(128)S(1)}) all-reduce(f32[128]{0:T(128)S(1)} %get-tuple-element.17, f32[128]{0:T(128)S(1)} %get-tuple-element.15, f32[128]{0:T(128)S(1)} %get-tuple-element.13, f32[128]{0:T(128)S(1)} %get-tuple-element.11), channel_id=1, replica_groups=mesh['dom'=8,'case'=4] {'dom'}, use_global_device_ids=true, to_apply=%region_7.9 | all-reduce | flops 512 | bytes 4096 | tf_op jit(solution)/shard_map/psum | solution.py:124
  582.7 6.2 %pmax.7 = f32[4]{0:T(128)} all-reduce(f32[4]{0:T(128)S(1)} %get-tuple-element.9), channel_id=1, replica_groups=mesh['dom'=8,'case'=4] {'case'}, use_global_device_ids=true, to_apply=%region_9.11 | all-reduce | flops 4 | bytes 32 | tf_op jit(solution)/shard_map/pmax | solution.py:134
  (272 shorter events, 178.3 us)
Async XLA Ops:
  3.6 19.9 %collective-permute-start = (f32[768,128]{1,0:T(8,128)}, f32[768,128]{1,0:T(8,128)S(1)}, u32[]{:S(2)}, u32[]{:S(2)}) collective-permute-start(f32[768,128]{1,0:T(8,128)} %get-tuple-element.44), channel_id=1, source_target_pairs={{28,0},{0,4},{4,8},{8,12},{12,16},{16,20},{20,24},{24,28},{29,1},{... | collective-permute-start | bytes 1179656 | tf_op jit(solution)/shard_map/ppermute | solution.py:29
  37.3 6.5 %collective-permute-start.6 = (bf16[2,16,128]{2,1,0:T(8,128)(2,1)S(1)}, bf16[2,16,128]{2,1,0:T(8,128)(2,1)S(1)}, u32[]{:S(2)}, u32[]{:S(2)}) collective-permute-start(bf16[2,16,128]{2,1,0:T(8,128)(2,1)S(1)} %collective-permute-done.5), channel_id=1, source_target_pairs={{0,28},{4,0},{8,4},{12,8},{16,12},{20,16},{24,20},{28,24},{1,29},{... | collective-permute-start | bytes 24584 | tf_op jit(solution)/shard_map/ppermute | solution.py:21
  52.5 10.0 %collective-permute-start.8 = (f32[768,128]{1,0:T(8,128)S(1)}, f32[768,128]{1,0:T(8,128)S(1)}, u32[]{:S(2)}, u32[]{:S(2)}) collective-permute-start(f32[768,128]{1,0:T(8,128)S(1)} %get-tuple-element.34), channel_id=1, source_target_pairs={{4,0},{8,4},{12,8},{16,12},{20,16},{24,20},{28,24},{0,28},{5,1},{9... | collective-permute-start | bytes 1179656 | tf_op jit(solution)/shard_map/ppermute | solution.py:29
  64.9 160.3 %collective-permute-start.9 = (f32[768,128]{1,0:T(8,128)S(1)}, f32[768,128]{1,0:T(8,128)S(1)}, u32[]{:S(2)}, u32[]{:S(2)}) collective-permute-start(f32[768,128]{1,0:T(8,128)S(1)} %get-tuple-element.42), channel_id=1, source_target_pairs={{28,0},{0,4},{4,8},{8,12},{12,16},{16,20},{20,24},{24,28},{29,1},{... | collective-permute-start | bytes 1179656 | tf_op jit(solution)/shard_map/ppermute | solution.py:29
  65.1 160.1 %collective-permute-start.16 = (s32[9]{0:T(128)S(1)}, s32[9]{0:T(128)S(1)}, u32[]{:S(2)}, u32[]{:S(2)}) collective-permute-start(s32[9]{0:T(128)S(1)} %get-tuple-element.51), channel_id=1, source_target_pairs={{4,0},{8,4},{12,8},{16,12},{20,16},{24,20},{28,24},{0,28},{5,1},{9... | collective-permute-start | bytes 116 | tf_op jit(solution)/shard_map/ppermute | solution.py:29
  70.4 154.8 %collective-permute-start.15 = (s32[9]{0:T(128)S(1)}, s32[9]{0:T(128)S(1)}, u32[]{:S(2)}, u32[]{:S(2)}) collective-permute-start(s32[9]{0:T(128)S(1)} %get-tuple-element.50), channel_id=1, source_target_pairs={{28,0},{0,4},{4,8},{8,12},{12,16},{16,20},{20,24},{24,28},{29,1},{... | collective-permute-start | bytes 116 | tf_op jit(solution)/shard_map/ppermute | solution.py:29
  258.5 11.3 %collective-permute-start.10 = (f32[768,128]{1,0:T(8,128)S(1)}, f32[768,128]{1,0:T(8,128)S(1)}, u32[]{:S(2)}, u32[]{:S(2)}) collective-permute-start(f32[768,128]{1,0:T(8,128)S(1)} %get-tuple-element.31), channel_id=1, source_target_pairs={{4,0},{8,4},{12,8},{16,12},{20,16},{24,20},{28,24},{0,28},{5,1},{9... | collective-permute-start | bytes 1179656 | tf_op jit(solution)/shard_map/ppermute | solution.py:29
  263.5 10.6 %collective-permute-start.17 = (f32[768,128]{1,0:T(8,128)S(1)}, f32[768,128]{1,0:T(8,128)S(1)}, u32[]{:S(2)}, u32[]{:S(2)}) collective-permute-start(f32[768,128]{1,0:T(8,128)S(1)} %get-tuple-element.30), channel_id=1, source_target_pairs={{28,0},{0,4},{4,8},{8,12},{12,16},{16,20},{20,24},{24,28},{29,1},{... | collective-permute-start | bytes 1179656 | tf_op jit(solution)/shard_map/ppermute | solution.py:29
  275.4 6.5 %collective-permute-start.18 = (bf16[2,16,128]{2,1,0:T(8,128)(2,1)S(1)}, bf16[2,16,128]{2,1,0:T(8,128)(2,1)S(1)}, u32[]{:S(2)}, u32[]{:S(2)}) collective-permute-start(bf16[2,16,128]{2,1,0:T(8,128)(2,1)S(1)} %fusion.27), channel_id=1, source_target_pairs={{0,4},{4,8},{8,12},{12,16},{16,20},{20,24},{24,28},{28,0},{1,5},{5... | collective-permute-start | bytes 24584 | tf_op jit(solution)/shard_map/ppermute | solution.py:19
  281.9 6.5 %collective-permute-start.19 = (bf16[2,16,128]{2,1,0:T(8,128)(2,1)S(1)}, bf16[2,16,128]{2,1,0:T(8,128)(2,1)}, u32[]{:S(2)}, u32[]{:S(2)}) collective-permute-start(bf16[2,16,128]{2,1,0:T(8,128)(2,1)S(1)} %collective-permute-done.18), channel_id=1, source_target_pairs={{0,4},{4,8},{8,12},{12,16},{16,20},{20,24},{24,28},{28,0},{1,5},{5... | collective-permute-start | bytes 24584 | tf_op jit(solution)/shard_map/ppermute | solution.py:19
  281.9 12.2 %collective-permute-start.22 = (bf16[2,16,128]{2,1,0:T(8,128)(2,1)S(1)}, bf16[2,16,128]{2,1,0:T(8,128)(2,1)}, u32[]{:S(2)}, u32[]{:S(2)}) collective-permute-start(bf16[2,16,128]{2,1,0:T(8,128)(2,1)S(1)} %fusion.27), channel_id=1, source_target_pairs={{0,28},{4,0},{8,4},{12,8},{16,12},{20,16},{24,20},{28,24},{1,29},{... | collective-permute-start | bytes 24584 | tf_op jit(solution)/shard_map/ppermute | solution.py:21
  288.4 10.4 %collective-permute-start.20 = (bf16[2,16,128]{2,1,0:T(8,128)(2,1)}, bf16[2,16,128]{2,1,0:T(8,128)(2,1)}, u32[]{:S(2)}, u32[]{:S(2)}) collective-permute-start(bf16[2,16,128]{2,1,0:T(8,128)(2,1)} %collective-permute-done.19), channel_id=1, source_target_pairs={{0,4},{4,8},{8,12},{12,16},{16,20},{20,24},{24,28},{28,0},{1,5},{5... | collective-permute-start | bytes 24584 | tf_op jit(solution)/shard_map/ppermute | solution.py:19
  289.1 21.8 %collective-permute-start.14 = (f32[8,16,16]{2,1,0:T(8,128)}, f32[8,16,16]{2,1,0:T(8,128)S(1)}, u32[]{:S(2)}, u32[]{:S(2)}) collective-permute-start(f32[8,16,16]{2,1,0:T(8,128)} %get-tuple-element.47), channel_id=1, source_target_pairs={{4,0},{8,4},{12,8},{16,12},{20,16},{24,20},{28,24},{0,28},{5,1},{9... | collective-permute-start | bytes 24584 | tf_op jit(solution)/shard_map/ppermute | solution.py:29
  293.8 17.1 %collective-permute-start.13 = (f32[8,16,16]{2,1,0:T(8,128)}, f32[8,16,16]{2,1,0:T(8,128)S(1)}, u32[]{:S(2)}, u32[]{:S(2)}) collective-permute-start(f32[8,16,16]{2,1,0:T(8,128)} %get-tuple-element.46), channel_id=1, source_target_pairs={{28,0},{0,4},{4,8},{8,12},{12,16},{16,20},{20,24},{24,28},{29,1},{... | collective-permute-start | bytes 24584 | tf_op jit(solution)/shard_map/ppermute | solution.py:29
  294.0 9.6 %collective-permute-start.23 = (bf16[2,16,128]{2,1,0:T(8,128)(2,1)}, bf16[2,16,128]{2,1,0:T(8,128)(2,1)S(1)}, u32[]{:S(2)}, u32[]{:S(2)}) collective-permute-start(bf16[2,16,128]{2,1,0:T(8,128)(2,1)} %collective-permute-done.22), channel_id=1, source_target_pairs={{0,28},{4,0},{8,4},{12,8},{16,12},{20,16},{24,20},{28,24},{1,29},{... | collective-permute-start | bytes 24584 | tf_op jit(solution)/shard_map/ppermute | solution.py:21
  298.8 6.6 %collective-permute-start.21 = (bf16[2,16,128]{2,1,0:T(8,128)(2,1)}, bf16[2,16,128]{2,1,0:T(8,128)(2,1)S(1)}, u32[]{:S(2)}, u32[]{:S(2)}) collective-permute-start(bf16[2,16,128]{2,1,0:T(8,128)(2,1)} %collective-permute-done.20), channel_id=1, source_target_pairs={{0,4},{4,8},{8,12},{12,16},{16,20},{20,24},{24,28},{28,0},{1,5},{5... | collective-permute-start | bytes 24584 | tf_op jit(solution)/shard_map/ppermute | solution.py:19
  298.8 12.7 %collective-permute-start.12 = (bf16[16,1536]{1,0:T(8,128)(2,1)S(1)}, bf16[16,1536]{1,0:T(8,128)(2,1)S(1)}, u32[]{:S(2)}, u32[]{:S(2)}) collective-permute-start(bf16[16,1536]{1,0:T(8,128)(2,1)S(1)} %get-tuple-element.49), channel_id=1, source_target_pairs={{4,0},{8,4},{12,8},{16,12},{20,16},{24,20},{28,24},{0,28},{5,1},{9... | collective-permute-start | bytes 147464 | tf_op jit(solution)/shard_map/ppermute | solution.py:29
  303.6 7.9 %collective-permute-start.11 = (bf16[16,1536]{1,0:T(8,128)(2,1)S(1)}, bf16[16,1536]{1,0:T(8,128)(2,1)S(1)}, u32[]{:S(2)}, u32[]{:S(2)}) collective-permute-start(bf16[16,1536]{1,0:T(8,128)(2,1)S(1)} %get-tuple-element.48), channel_id=1, source_target_pairs={{28,0},{0,4},{4,8},{8,12},{12,16},{16,20},{20,24},{24,28},{29,1},{... | collective-permute-start | bytes 147464 | tf_op jit(solution)/shard_map/ppermute | solution.py:29
  350.2 9.5 %collective-permute-start.25 = (f32[768,128]{1,0:T(8,128)S(1)}, f32[768,128]{1,0:T(8,128)S(1)}, u32[]{:S(2)}, u32[]{:S(2)}) collective-permute-start(f32[768,128]{1,0:T(8,128)S(1)} %get-tuple-element.28), channel_id=1, source_target_pairs={{4,0},{8,4},{12,8},{16,12},{20,16},{24,20},{28,24},{0,28},{5,1},{9... | collective-permute-start | bytes 1179656 | tf_op jit(solution)/shard_map/ppermute | solution.py:29
  354.4 10.6 %collective-permute-start.26 = (f32[768,128]{1,0:T(8,128)S(1)}, f32[768,128]{1,0:T(8,128)S(1)}, u32[]{:S(2)}, u32[]{:S(2)}) collective-permute-start(f32[768,128]{1,0:T(8,128)S(1)} %get-tuple-element.27), channel_id=1, source_target_pairs={{28,0},{0,4},{4,8},{8,12},{12,16},{16,20},{20,24},{24,28},{29,1},{... | collective-permute-start | bytes 1179656 | tf_op jit(solution)/shard_map/ppermute | solution.py:29
  432.3 10.0 %collective-permute-start.34 = (f32[768,128]{1,0:T(8,128)S(1)}, f32[768,128]{1,0:T(8,128)S(1)}, u32[]{:S(2)}, u32[]{:S(2)}) collective-permute-start(f32[768,128]{1,0:T(8,128)S(1)} %get-tuple-element.25), channel_id=1, source_target_pairs={{4,0},{8,4},{12,8},{16,12},{20,16},{24,20},{28,24},{0,28},{5,1},{9... | collective-permute-start | bytes 1179656 | tf_op jit(solution)/shard_map/ppermute | solution.py:29
  437.0 10.6 %collective-permute-start.35 = (f32[768,128]{1,0:T(8,128)S(1)}, f32[768,128]{1,0:T(8,128)S(1)}, u32[]{:S(2)}, u32[]{:S(2)}) collective-permute-start(f32[768,128]{1,0:T(8,128)S(1)} %get-tuple-element.24), channel_id=1, source_target_pairs={{28,0},{0,4},{4,8},{8,12},{12,16},{16,20},{20,24},{24,28},{29,1},{... | collective-permute-start | bytes 1179656 | tf_op jit(solution)/shard_map/ppermute | solution.py:29
  512.6 10.1 %collective-permute-start.43 = (f32[768,128]{1,0:T(8,128)S(1)}, f32[768,128]{1,0:T(8,128)S(1)}, u32[]{:S(2)}, u32[]{:S(2)}) collective-permute-start(f32[768,128]{1,0:T(8,128)S(1)} %get-tuple-element.22), channel_id=1, source_target_pairs={{4,0},{8,4},{12,8},{16,12},{20,16},{24,20},{28,24},{0,28},{5,1},{9... | collective-permute-start | bytes 1179656 | tf_op jit(solution)/shard_map/ppermute | solution.py:29
  517.3 10.5 %collective-permute-start.44 = (f32[768,128]{1,0:T(8,128)S(1)}, f32[768,128]{1,0:T(8,128)S(1)}, u32[]{:S(2)}, u32[]{:S(2)}) collective-permute-start(f32[768,128]{1,0:T(8,128)S(1)} %get-tuple-element.21), channel_id=1, source_target_pairs={{28,0},{0,4},{4,8},{8,12},{12,16},{16,20},{20,24},{24,28},{29,1},{... | collective-permute-start | bytes 1179656 | tf_op jit(solution)/shard_map/ppermute | solution.py:29
  (58 other events, 642.6 us)
